TPU v7x, 32 devices: a whole 2x2x4 slice. The times are simulated.
32 devices in a mesh: grp: 2 (over y), ep: 4 (over z), tp: 2 (over x), mb: 2 (over core).
Axes of the slice: x: 2, y: 2, z: 4, core: 2. Of those that a mesh axis runs over, the one named last changes fastest.
Arguments:
- hidden: bfloat16 [256, 3584], P(('grp', 'ep', 'mb'), 'tp'), parts along dimension 0, may hold values from -12 to 12
- moe_gain: float32 [3584], P('tp'), may hold values from 0.1 to 1.9
- expert_ids: int32 [256, 8], P(('grp', 'ep', 'mb')), parts along dimension 0, may hold values from 0 to 7, as said below
- slots: int32 [256, 8], P(('grp', 'ep', 'mb')), parts along dimension 0, may hold values from 0 to 15, as said below
- affinity: float32 [256, 8], P(('grp', 'ep', 'mb')), parts along dimension 0, may hold values from 0.05 to 1
- w_gate: bfloat16 [8, 3584, 1024], P(('ep', 'mb'), None, 'tp'), may hold values from -0.09375 to 0.09375
- w_up: bfloat16 [8, 3584, 1024], P(('ep', 'mb'), None, 'tp'), may hold values from -0.09375 to 0.09375
- w_down: bfloat16 [8, 1024, 3584], P(('ep', 'mb'), 'tp'), may hold values from -0.1875 to 0.1875
- attn_gain: float32 [3584], P('tp'), may hold values from 0.1 to 1.9
- w_dkv: bfloat16 [3584, 576], P('tp'), may hold values from -0.09375 to 0.09375
- kv_gain: float32 [512], replicated, may hold values from 0.1 to 1.9
- queries: bfloat16 [256, 64, 576], P(('grp', 'ep', 'mb'), 'tp'), parts along dimension 0, may hold values from -36 to 36
- cache: bfloat16 [256, 128, 576], P(('grp', 'ep', 'mb'), 'tp'), parts along dimension 0, may hold values from -4 to 4
- lengths: int32 [256], P(('grp', 'ep', 'mb')), parts along dimension 0, may hold values from 2 to 128
Outputs:
- next_hidden: bfloat16 [256, 3584], P(('grp', 'ep', 'mb'), 'tp'), parts along dimension 0
- latent_out: bfloat16 [256, 64, 512], P(('grp', 'ep', 'mb'), 'tp'), parts along dimension 0
There are 2 independent parts, one for each index of `grp`. A program takes and returns all parts, laid end to end along the dimension named above; an argument that names none is the same for every part. Nothing has to cross between parts.
Inputs may be any that keep to these rules, and one draw needn't show every extreme that they name: `expert_ids`: each row names 8 different experts; in every draw some expert is named by every token. slots[t, k] is the rank of the choice (t, k) among the choices of the same expert made by the 16 tokens of one device; these ranks are distinct and run from 0 upward. A choice whose slot is 8 or more is dropped.
All inputs are finite; a program needn't handle non-finite values.
Results may differ from a plain program's by a relative error of at most 0.017.
Values may be sent and summed in bfloat16 or wider, within the bound.
A program may use at most 128 MiB of HBM per device.

v0:
```python
import jax
import jax.numpy as jnp
from jax import lax
from jax.sharding import PartitionSpec as P

D = 3584
LAT = 512
CAP = 8


epsilon = 1e-06
route_scale = 2.5
score_scale = 192.0 ** (-0.5)


def rope_rotate(rope_part, position):
    half_rope = rope_part.shape[-1] // 2
    inv_freq = 10000.0 ** (-jnp.arange(half_rope, dtype=jnp.float32) / half_rope)
    angles = position[:, None] * inv_freq[None, :]
    cos_table = jnp.cos(angles)
    sin_table = jnp.sin(angles)
    first_half = rope_part[:, :half_rope]
    second_half = rope_part[:, half_rope:]
    return jnp.concatenate(
        [
            first_half * cos_table - second_half * sin_table,
            first_half * sin_table + second_half * cos_table,
        ],
        1,
    )


def local(
    hidden,
    moe_gain,
    expert_ids,
    slots,
    affinity,
    w_gate,
    w_up,
    w_down,
    attn_gain,
    w_dkv,
    kv_gain,
    queries,
    cache,
    lengths,
):
    experts = lax.axis_size("ep") * lax.axis_size("mb")
    slot_rows = experts * CAP
    hidden_wide = hidden.astype(jnp.float32)
    square = lax.psum(jnp.sum(hidden_wide * hidden_wide, -1), "tp")
    normed = (hidden_wide * lax.rsqrt(square[:, None] / D + epsilon) * moe_gain).astype(
        jnp.bfloat16
    )
    kept_rows = slots < CAP
    weight = (
        route_scale
        * affinity
        / jnp.sum(affinity, -1, keepdims=True)
        * kept_rows.astype(jnp.float32)
    )
    target = jnp.where(kept_rows, expert_ids * CAP + slots, -1)
    matches = target[None, :, :] == jnp.arange(slot_rows, dtype=jnp.int32)[:, None, None]
    dispatch = jnp.any(matches, 2).astype(jnp.bfloat16)
    combine = jnp.sum(jnp.where(matches, weight[None, :, :], 0.0), 2).T
    gate_weight = w_gate[0]
    up_weight = w_up[0]
    down_weight = w_down[0]
    full_rows = lax.all_gather(normed, "tp", axis=1, tiled=True)
    send_rows = jnp.dot(dispatch, full_rows, preferred_element_type=jnp.float32).astype(
        jnp.bfloat16
    )
    arrived = lax.all_to_all(
        send_rows.reshape(experts, CAP, D), ("ep", "mb"), split_axis=0, concat_axis=0, tiled=True
    ).reshape(slot_rows, D)
    gate_act = jnp.dot(arrived, gate_weight, preferred_element_type=jnp.float32)
    up_act = jnp.dot(arrived, up_weight, preferred_element_type=jnp.float32)
    units = (jax.nn.silu(gate_act) * up_act).astype(jnp.bfloat16)
    partial_out = jnp.dot(units, down_weight, preferred_element_type=jnp.float32)
    returned = lax.all_to_all(
        partial_out.astype(jnp.bfloat16).reshape(experts, CAP, D),
        ("ep", "mb"),
        split_axis=0,
        concat_axis=0,
        tiled=True,
    ).reshape(slot_rows, D)
    token_sums = jnp.dot(combine, returned.astype(jnp.float32), precision=lax.Precision.HIGHEST)
    moe_out = lax.psum_scatter(
        token_sums.astype(jnp.bfloat16), "tp", scatter_dimension=1, tiled=True
    ).astype(jnp.float32)
    next_hidden = (hidden_wide + moe_out).astype(jnp.bfloat16)
    next_wide = next_hidden.astype(jnp.float32)
    square_attn = lax.psum(jnp.sum(next_wide * next_wide, -1), "tp")
    normed_attn = (next_wide * lax.rsqrt(square_attn[:, None] / D + epsilon) * attn_gain).astype(
        jnp.bfloat16
    )
    down_kv = lax.psum(
        jnp.dot(normed_attn, w_dkv, preferred_element_type=jnp.float32).astype(jnp.bfloat16), "tp"
    ).astype(jnp.float32)
    latent_part = down_kv[:, :LAT]
    latent_part = (
        latent_part
        * lax.rsqrt(jnp.mean(latent_part * latent_part, -1, keepdims=True) + epsilon)
        * kv_gain
    )
    rope_part = rope_rotate(down_kv[:, LAT:], lengths.astype(jnp.float32))
    new_key = jnp.concatenate([latent_part, rope_part], 1).astype(jnp.bfloat16)
    own_score = (
        jnp.einsum("bhc,bc->bh", queries, new_key, preferred_element_type=jnp.float32) * score_scale
    )
    all_queries = lax.all_gather(queries, "tp", axis=1, tiled=True)
    span_len = cache.shape[1]
    first_pos = lax.axis_index("tp") * span_len
    position = first_pos + jnp.arange(span_len, dtype=jnp.int32)
    live_mask = (position[None, :] < lengths[:, None])[:, None, :]
    scores = (
        jnp.einsum("bhc,bjc->bhj", all_queries, cache, preferred_element_type=jnp.float32)
        * score_scale
    )
    scores = jnp.where(live_mask, scores, -1e30)
    peak_local = jnp.max(scores, -1)
    prob_live = jnp.where(live_mask, jnp.exp(scores - peak_local[:, :, None]), 0.0)
    mass_local = jnp.sum(prob_live, -1)
    accumulated = jnp.einsum(
        "bhj,bjc->bhc",
        prob_live.astype(jnp.bfloat16),
        cache[:, :, :LAT],
        preferred_element_type=jnp.float32,
    )
    peaks, masses, accums = (
        lax.all_to_all(
            peak_local[None].astype(jnp.bfloat16), "tp", split_axis=2, concat_axis=0, tiled=True
        ).astype(jnp.float32),
        lax.all_to_all(
            mass_local[None].astype(jnp.bfloat16), "tp", split_axis=2, concat_axis=0, tiled=True
        ).astype(jnp.float32),
        lax.all_to_all(
            accumulated[None].astype(jnp.bfloat16), "tp", split_axis=2, concat_axis=0, tiled=True
        ).astype(jnp.float32),
    )
    peak_all = jnp.maximum(jnp.max(peaks, 0), own_score)
    factor = jnp.exp(peaks - peak_all[None])
    own_prob = jnp.exp(own_score - peak_all)
    denominator = jnp.sum(masses * factor, 0) + own_prob
    numerator = jnp.sum(accums * factor[:, :, :, None], 0)
    numerator = numerator + own_prob.astype(jnp.bfloat16).astype(jnp.float32)[:, :, None] * new_key[
        :, None, :LAT
    ].astype(jnp.float32)
    latent_out = (numerator / denominator[:, :, None]).astype(jnp.bfloat16)
    return (next_hidden, latent_out)


def solution(mesh):
    return jax.shard_map(
        local,
        mesh=mesh,
        in_specs=(
            P(("grp", "ep", "mb"), "tp"),
            P("tp"),
            P(("grp", "ep", "mb"), None),
            P(("grp", "ep", "mb"), None),
            P(("grp", "ep", "mb"), None),
            P(("ep", "mb"), None, "tp"),
            P(("ep", "mb"), None, "tp"),
            P(("ep", "mb"), "tp", None),
            P("tp"),
            P("tp", None),
            P(),
            P(("grp", "ep", "mb"), "tp", None),
            P(("grp", "ep", "mb"), "tp", None),
            P(("grp", "ep", "mb")),
        ),
        out_specs=(P(("grp", "ep", "mb"), "tp"), P(("grp", "ep", "mb"), "tp", None)),
        check_vma=False,
    )
```

profile of v0, /device:TPU:0, one launch (start us, length us, event | category | flops | bytes accessed | tf_op | source)
XLA Modules:
  0.0 115.2 jit_solution(4110498424338626534)
XLA Ops:
  7.2 0.0 copy-start
  7.2 0.0 copy-start.3
  7.2 1.1 fusion.37
  8.3 5.9 %psum.21 = f32[16]{0:T(128)S(1)} all-reduce(f32[16]{0:T(128)S(1)} %fusion.37), channel_id=1, replica_groups=mesh['grp'=2,'ep'=4,'tp'=2,'mb'=2] {'tp'}, use_global_device_ids=true, to_apply=%region_4.5 | all-reduce | flops 16 | bytes 128 | tf_op jit(solution)/shard_map/psum | solution.py:52
  14.2 0.7 add_select_fusion
  14.9 0.1 copy.69
  15.0 0.1 fusion.42
  15.1 0.9 fusion.39
  16.0 4.8 %all_gather.6 = bf16[16,3584]{1,0:T(8,128)(2,1)S(1)} all-gather(bf16[16,1792]{1,0:T(8,128)(2,1)S(1)} %fusion.39), channel_id=1, replica_groups=mesh['grp'=2,'ep'=4,'tp'=2,'mb'=2] {'tp'}, dimensions={1}, use_global_device_ids=true | all-gather | bytes 172032 | tf_op jit(solution)/shard_map/all_gather | solution.py:70
  20.8 1.1 fusion
  21.9 5.4 %all-to-all-start = ((bf16[8,8,3584]{2,1,0:T(8,128)(2,1)}), bf16[8,8,3584]{2,1,0:T(8,128)(2,1)S(1)}, u32[]{:S(2)}, u32[]{:S(2)}) async-start(bf16[8,8,3584]{2,1,0:T(8,128)(2,1)} %fusion), calls=%async_computation | async-start | bytes 917504 | tf_op jit(solution)/shard_map/all_to_all | solution.py:74
  27.3 0.0 all-gather.2.cloned.1.call-start
  27.4 0.7 all-gather.2.cloned.1.call-update
  28.1 0.1 broadcast_compare_fusion
  28.2 13.0 %all-to-all-done = bf16[8,8,3584]{2,1,0:T(8,128)(2,1)S(1)} async-done(((bf16[8,8,3584]{2,1,0:T(8,128)(2,1)}), bf16[8,8,3584]{2,1,0:T(8,128)(2,1)S(1)}, u32[]{:S(2)}, u32[]{:S(2)}) %all-to-all-start) | async-done | bytes 458784 | tf_op jit(solution)/shard_map/all_to_all | solution.py:74
  41.3 2.8 %fusion.5 = f32[64,512]{1,0:T(8,128)S(1)} fusion(bf16[1,3584,512]{2,1,0:T(8,128)(2,1)} %param.19, bf16[8,8,3584]{2,1,0:T(8,128)(2,1)S(1)} %all-to-all-done), kind=kOutput, calls=%fused_computation.8 | convolution fusion | flops 234881024 | bytes 4259840 | tf_op jit(solution)/shard_map/dot_general | solution.py:77
  44.0 5.4 %fusion.1 = bf16[8,8,3584]{2,1,0:T(8,128)(2,1)} fusion(bf16[1,512,3584]{2,1,0:T(8,128)(2,1)} %param.21, bf16[1,3584,512]{2,1,0:T(8,128)(2,1)} %param.20, bf16[8,8,3584]{2,1,0:T(8,128)(2,1)S(1)} %all-to-all-done, f32[64,512]{1,0:T(8,128)S(1)} %fusion.5), kind=kOutput, calls=%fused_computation.3 | convolution fusion | flops 470188032 | bytes 8388608 | tf_op jit(solution)/shard_map/dot_general | solution.py:80
  49.4 3.5 %all-to-all-start.1 = ((bf16[8,8,3584]{2,1,0:T(8,128)(2,1)}), bf16[8,8,3584]{2,1,0:T(8,128)(2,1)S(1)}, u32[]{:S(2)}, u32[]{:S(2)}) async-start(bf16[8,8,3584]{2,1,0:T(8,128)(2,1)} %fusion.1), calls=%async_computation.1 | async-start | bytes 917504 | tf_op jit(solution)/shard_map/all_to_all | solution.py:81
  52.9 0.1 copy.70
  53.0 0.1 select_reduce_fusion
  53.1 2.3 %all-gather.2.cloned.1.call-done = bf16[16,64,576]{2,1,0:T(8,128)(2,1)} async-done(((bf16[16,32,576]{2,1,0:T(8,128)(2,1)}), bf16[16,64,576]{2,1,0:T(8,128)(2,1)}) %all-gather.2.cloned.1.call-update) | async-done | bytes 1179664 | tf_op jit(solution)/shard_map/all_gather | solution.py:112
  55.4 2.3 %fusion.63 = (f32[16,64]{1,0:T(8,128)S(1)}, f32[16,64,64]{1,2,0:T(8,128)S(1)}) fusion(bf16[16,64,576]{2,1,0:T(8,128)(2,1)} %all-gather.2.cloned.1.call-done, bf16[16,64,576]{2,1,0:T(8,128)(2,1)} %param.26, pred[16,64]{1,0:T(8,128)(4,1)S(1)} %broadcast_compare_fusion), kind=kOutput, calls=%fused_computation.91 | convolution fusion | flops 75693056 | bytes 2626560 | tf_op jit(solution)/shard_map/bhc,bjc->bhj/dot_general | solution.py:118
  57.7 0.1 copy.73
  57.8 0.5 broadcast.98
  58.3 0.7 reduce.3
  59.1 0.7 reshape.127
  59.7 0.2 fusion.23
  60.0 0.1 copy.77
  60.1 0.7 reduce.2
  60.8 0.7 reshape.125
  61.5 5.2 %all-to-all-done.1 = bf16[8,8,3584]{2,1,0:T(8,128)(2,1)S(1)} async-done(((bf16[8,8,3584]{2,1,0:T(8,128)(2,1)}), bf16[8,8,3584]{2,1,0:T(8,128)(2,1)S(1)}, u32[]{:S(2)}, u32[]{:S(2)}) %all-to-all-start.1) | async-done | bytes 458784 | tf_op jit(solution)/shard_map/all_to_all | solution.py:81
  66.7 3.2 %all-to-all-start.4 = ((bf16[2,2,256]{2,1,0:T(2,128)(2,1)}), bf16[2,2,256]{2,1,0:T(2,128)(2,1)S(1)}, u32[]{:S(2)}, u32[]{:S(2)}) async-start(bf16[2,2,256]{2,1,0:T(2,128)(2,1)} %reshape.125), calls=%async_computation.5 | async-start | bytes 4096 | tf_op jit(solution)/shard_map/all_to_all | solution.py:135
  70.0 0.0 reduce-scatter.2.cloned.1.call-start
  70.0 0.9 convolution_convert_fusion.2
  71.0 0.0 reduce-scatter.2.cloned.1.call-update
  71.0 2.7 %all-to-all-done.4 = bf16[2,2,256]{2,1,0:T(2,128)(2,1)S(1)} async-done(((bf16[2,2,256]{2,1,0:T(2,128)(2,1)}), bf16[2,2,256]{2,1,0:T(2,128)(2,1)S(1)}, u32[]{:S(2)}, u32[]{:S(2)}) %all-to-all-start.4) | async-done | bytes 2080 | tf_op jit(solution)/shard_map/all_to_all | solution.py:135
  73.7 3.2 %all-to-all-start.3 = ((bf16[2,2,256]{2,1,0:T(2,128)(2,1)}), bf16[2,2,256]{2,1,0:T(2,128)(2,1)S(1)}, u32[]{:S(2)}, u32[]{:S(2)}) async-start(bf16[2,2,256]{2,1,0:T(2,128)(2,1)} %reshape.127), calls=%async_computation.4 | async-start | bytes 4096 | tf_op jit(solution)/shard_map/all_to_all | solution.py:132
  76.9 2.0 %fusion.8 = bf16[1,16,64,512]{3,2,1,0:T(8,128)(2,1)S(1)} fusion(bf16[16,64,576]{2,1,0:T(8,128)(2,1)} %param.26, f32[16,64,64]{1,2,0:T(8,128)S(1)} %get-tuple-element.21, f32[16,64]{1,0:T(8,128)S(1)} %get-tuple-element.20, pred[16,64]{1,0:T(8,128)(4,1)S(1)} %broadcast_compare_fusion), kind=kOutput, calls=%fused_computation.13 | convolution fusion | flops 67829760 | bytes 2364416 | tf_op jit(solution)/shard_map/bhj,bjc->bhc/dot_general | solution.py:125
  78.9 0.0 copy-start.1
  78.9 1.6 %copy.72 = bf16[1,16,64,512]{3,1,0,2:T(8,128)(2,1)} copy(bf16[1,16,64,512]{3,2,1,0:T(8,128)(2,1)S(1)} %fusion.8) | data formatting | bytes 2097152 | tf_op jit(solution)/shard_map/convert_element_type | solution.py:139
  80.5 0.1 reshape.126
  80.6 0.1 copy.78
  80.7 0.1 reshape.122
  80.8 3.6 %all-to-all-start.2 = ((bf16[1,16,64,512]{3,1,0,2:T(8,128)(2,1)}), bf16[1,16,64,512]{3,1,0,2:T(8,128)(2,1)S(1)}, u32[]{:S(2)}, u32[]{:S(2)}) async-start(bf16[1,16,64,512]{3,1,0,2:T(8,128)(2,1)} %copy.72), calls=%async_computation.3 | async-start | bytes 2097152 | tf_op jit(solution)/shard_map/all_to_all | solution.py:138
  84.4 0.1 reshape.128
  84.5 0.1 copy.74
  84.6 0.1 all_to_all.35
  84.7 0.0 reduce-scatter.2.cloned.1.call-done
  84.7 1.0 fusion.34
  85.7 11.2 %psum.22 = f32[16]{0:T(128)S(1)} all-reduce(f32[16]{0:T(128)S(1)} %get-tuple-element.12), channel_id=1, replica_groups=mesh['grp'=2,'ep'=4,'tp'=2,'mb'=2] {'tp'}, use_global_device_ids=true, to_apply=%region_9.10 | all-reduce | flops 16 | bytes 128 | tf_op jit(solution)/shard_map/psum | solution.py:94
  96.9 0.6 convolution_convert_fusion.4
  97.6 7.1 %psum.23 = bf16[16,576]{1,0:T(8,128)(2,1)S(1)} all-reduce(bf16[16,576]{1,0:T(8,128)(2,1)S(1)} %convolution_convert_fusion.4), channel_id=1, replica_groups=mesh['grp'=2,'ep'=4,'tp'=2,'mb'=2] {'tp'}, use_global_device_ids=true, to_apply=%region_10.11 | all-reduce | flops 9216 | bytes 36864 | tf_op jit(solution)/shard_map/psum | solution.py:98
  104.6 0.1 multiply_reduce_fusion
  104.8 0.1 fusion.55
  104.9 0.1 fusion.61
  105.0 0.1 maximum_bitcast_fusion
  105.1 1.4 %fusion.46 = f32[16,1,32]{2,1,0:T(1,128)S(1)} fusion(bf16[16,32,576]{2,1,0:T(8,128)(2,1)} %param.25, bf16[16,576,1]{1,0,2:T(8,128)(2,1)S(1)} %maximum_bitcast_fusion), kind=kOutput, calls=%fused_computation.53 | convolution fusion | flops 589824 | bytes 610304 | tf_op jit(solution)/shard_map/bhc,bc->bh/dot_general | solution.py:110
  106.5 0.1 fusion.48
  106.5 0.1 copy.76
  106.6 0.1 copy.79
  106.7 0.1 copy.75
  106.8 0.2 fusion.7
  107.0 0.2 divide_convert_fusion
  107.3 1.1 copy.80
  (28 shorter events, 0.2 us)
Async XLA Ops:
  7.2 89.7 %copy-start = (bf16[1792,576]{0,1:T(8,128)(2,1)S(1)}, bf16[1792,576]{0,1:T(8,128)(2,1)}, u32[]{:S(2)}) copy-start(bf16[1792,576]{0,1:T(8,128)(2,1)} %param.23) | copy-start | bytes 6193156
  7.2 20.9 %copy-start.3 = (s32[16,8]{0,1:T(8,128)S(1)}, s32[16,8]{0,1:T(8,128)}, u32[]{:S(2)}) copy-start(s32[16,8]{0,1:T(8,128)} %param.17) | copy-start | bytes 1540
  7.2 20.9 %copy-start.4 = (f32[16,8]{0,1:T(8,128)S(1)}, f32[16,8]{0,1:T(8,128)}, u32[]{:S(2)}) copy-start(f32[16,8]{0,1:T(8,128)} %param.18) | copy-start | bytes 1540
  7.2 20.9 %copy-start.7 = (s32[16]{0:T(128)S(1)}, s32[16]{0:T(128)}, u32[]{:S(2)}) copy-start(s32[16]{0:T(128)} %param.27) | copy-start | bytes 196
  21.9 19.3 %all-to-all-start = ((bf16[8,8,3584]{2,1,0:T(8,128)(2,1)}), bf16[8,8,3584]{2,1,0:T(8,128)(2,1)S(1)}, u32[]{:S(2)}, u32[]{:S(2)}) async-start(bf16[8,8,3584]{2,1,0:T(8,128)(2,1)} %fusion), calls=%async_computation | async-start | bytes 917504 | tf_op jit(solution)/shard_map/all_to_all | solution.py:74
  27.3 28.1 %all-gather.2.cloned.1.call-start = ((), (), s32[]{:S(2)}) async-start(), calls=%async_computation.7 | async-start | bytes 1966080 | tf_op jit(solution)/shard_map/all_gather | solution.py:112
  49.4 17.3 %all-to-all-start.1 = ((bf16[8,8,3584]{2,1,0:T(8,128)(2,1)}), bf16[8,8,3584]{2,1,0:T(8,128)(2,1)S(1)}, u32[]{:S(2)}, u32[]{:S(2)}) async-start(bf16[8,8,3584]{2,1,0:T(8,128)(2,1)} %fusion.1), calls=%async_computation.1 | async-start | bytes 917504 | tf_op jit(solution)/shard_map/all_to_all | solution.py:81
  66.7 7.0 %all-to-all-start.4 = ((bf16[2,2,256]{2,1,0:T(2,128)(2,1)}), bf16[2,2,256]{2,1,0:T(2,128)(2,1)S(1)}, u32[]{:S(2)}, u32[]{:S(2)}) async-start(bf16[2,2,256]{2,1,0:T(2,128)(2,1)} %reshape.125), calls=%async_computation.5 | async-start | bytes 4096 | tf_op jit(solution)/shard_map/all_to_all | solution.py:135
  70.0 14.7 %reduce-scatter.2.cloned.1.call-start = ((), (), s32[]{:S(2)}) async-start(), calls=%async_computation.6 | async-start | bytes 172032 | tf_op jit(solution)/shard_map/reduce_scatter | solution.py:89
  73.7 7.0 %all-to-all-start.3 = ((bf16[2,2,256]{2,1,0:T(2,128)(2,1)}), bf16[2,2,256]{2,1,0:T(2,128)(2,1)S(1)}, u32[]{:S(2)}, u32[]{:S(2)}) async-start(bf16[2,2,256]{2,1,0:T(2,128)(2,1)} %reshape.127), calls=%async_computation.4 | async-start | bytes 4096 | tf_op jit(solution)/shard_map/all_to_all | solution.py:132
  78.9 5.8 %copy-start.1 = (bf16[16,1792]{1,0:T(8,128)(2,1)S(1)}, bf16[16,1792]{1,0:T(8,128)(2,1)}, u32[]{:S(2)}) copy-start(bf16[16,1792]{1,0:T(8,128)(2,1)} %param.14) | copy-start | bytes 172036
  78.9 18.0 %copy-start.5 = (f32[1792]{0:T(1024)S(1)}, f32[1792]{0:T(1024)}, u32[]{:S(2)}) copy-start(f32[1792]{0:T(1024)} %param.22) | copy-start | bytes 21508
  80.8 24.1 %copy-start.6 = (f32[512]{0:T(512)S(1)}, f32[512]{0:T(512)}, u32[]{:S(2)}) copy-start(f32[512]{0:T(512)} %param.24) | copy-start | bytes 6148
  80.8 26.0 %all-to-all-start.2 = ((bf16[1,16,64,512]{3,1,0,2:T(8,128)(2,1)}), bf16[1,16,64,512]{3,1,0,2:T(8,128)(2,1)S(1)}, u32[]{:S(2)}, u32[]{:S(2)}) async-start(bf16[1,16,64,512]{3,1,0,2:T(8,128)(2,1)} %copy.72), calls=%async_computation.3 | async-start | bytes 2097152 | tf_op jit(solution)/shard_map/all_to_all | solution.py:138
  85.7 21.3 %copy-start.2 = (bf16[16,1792]{1,0:T(8,128)(2,1)}, bf16[16,1792]{1,0:T(8,128)(2,1)S(1)}, u32[]{:S(2)}) copy-start(bf16[16,1792]{1,0:T(8,128)(2,1)S(1)} %get-tuple-element.13) | copy-start | bytes 172036
Sparse Core Ops, SparseCore 0:
  29.7 25.6 all-gather.1
  73.6 9.6 reduce-scatter.1
where the time goes:
time: 116 us; the launch traced here: 115 us
  blocking collectives  29 us (25%)
  waiting for transfers between devices  24 us (21%)
  starting transfers between devices  19 us (16%)
  matrix products  16.5 us (14%)
  between operations  14.3 us (12%)
  other arithmetic  6.73 us (6%)
  local copies, waits for them, and re-layouts  5.65 us (5%)
    all_to_all x1, waiting for transfers between devices, local(): lax.all_to_all(send_rows.reshape(experts, CAP, D), ('ep', 'mb'), split_ax...  13 us
    psum x1, blocking collectives, local(): square_attn = lax.psum(jnp.sum(next_wide * next_wide, -1), 'tp')  11.2 us
    psum x1, blocking collectives, local(): lax.psum(jnp.dot(normed_attn, w_dkv, preferred_element_type=jnp.float32)....  7.07 us
    psum x1, blocking collectives, local(): square = lax.psum(jnp.sum(hidden_wide * hidden_wide, -1), 'tp')  5.86 us
    all_to_all x1, starting transfers between devices, local(): lax.all_to_all(send_rows.reshape(experts, CAP, D), ('ep', 'mb'), split_ax...  5.4 us
    dot_general x1, matrix products, local(): jnp.dot(units, down_weight, preferred_element_type=jnp.float32)  5.39 us
    all_to_all x1, waiting for transfers between devices, local(): lax.all_to_all(partial_out.astype(jnp.bfloat16).reshape(experts, CAP, D),...  5.24 us
    all_gather x1, blocking collectives, local(): full_rows = lax.all_gather(normed, 'tp', axis=1, tiled=True)  4.85 us
  transfers between devices with their start and end apart: 7, of which 4 were waited for; matrix products, arithmetic and copies ran while one was open for 20% of the time, Pallas kernels for 0%

commit v1 on v0

v1 whole, which is shorter than its diff:
```python
import functools

import jax
import jax.numpy as jnp
from jax import lax
from jax.experimental import pallas as pl
from jax.experimental.pallas import tpu as pltpu
from jax.sharding import PartitionSpec as P

CAP = 8
GROUPS = 4
epsilon = 1e-06
route_scale = 2.5
score_scale = 192.0 ** (-0.5)
MESH = pl.DeviceIdType.MESH
F32 = jnp.float32
BF16 = jnp.bfloat16


def up(value, step):
    return -(-value // step) * step


def kernel(
    n_tp,
    n_ep,
    n_mb,
    hidden,
    moe_gain,
    ids,
    slots,
    affinity,
    w_gate,
    w_up,
    w_down,
    attn_gain,
    w_dkv,
    kv_gain,
    queries,
    cache,
    lengths,
    next_out,
    latent_out,
    hid_all,
    gain_all,
    send,
    arrived,
    wg,
    wu,
    wd,
    wk,
    ret_send,
    ret,
    tsum,
    rs_send,
    rs_recv,
    key_send,
    key_recv,
    q_buf,
    kv_buf,
    acc,
    peaks,
    masses,
    keys,
    load_sem,
    kv_load_sem,
    hid_ssem,
    hid_rsem,
    gain_ssem,
    gain_rsem,
    kv_ssem,
    kv_rsem,
    row_ssem,
    row_rsem,
    ret_ssem,
    ret_rsem,
    rs_ssem,
    rs_rsem,
    key_ssem,
    key_rsem,
):
    experts = n_ep * n_mb
    tokens, d_loc = hidden.shape
    d_all = d_loc * n_tp
    lat = kv_gain.shape[1]
    kvc = cache.shape[2]
    per_group = tokens // GROUPS
    tp = lax.axis_index("tp")
    me = lax.axis_index("ep") * n_mb + lax.axis_index("mb")

    def tp_id(step):
        return lax.rem(tp + step, n_tp)

    def ex_id(step):
        return lax.rem(me + step, experts)

    def ex_dev(index):
        return {"ep": index // n_mb, "mb": lax.rem(index, n_mb)}

    local = [
        pltpu.make_async_copy(hidden, hid_all.at[tp], load_sem.at[0]),
        pltpu.make_async_copy(moe_gain, gain_all.at[tp], load_sem.at[1]),
        pltpu.make_async_copy(queries, q_buf, load_sem.at[2]),
        pltpu.make_async_copy(w_gate.at[0], wg, load_sem.at[3]),
        pltpu.make_async_copy(w_up.at[0], wu, load_sem.at[4]),
        pltpu.make_async_copy(w_down.at[0], wd, load_sem.at[5]),
        pltpu.make_async_copy(w_dkv, wk, load_sem.at[6]),
    ]
    kv_load = pltpu.make_async_copy(cache, kv_buf.at[:, tp], kv_load_sem)
    local[0].start()
    local[1].start()

    barrier = pltpu.get_barrier_semaphore()
    for step in range(1, n_tp):
        pl.semaphore_signal(barrier, inc=1, device_id={"tp": tp_id(step)}, device_id_type=MESH)
    for step in range(1, experts):
        pl.semaphore_signal(barrier, inc=1, device_id=ex_dev(ex_id(step)), device_id_type=MESH)
    pl.semaphore_wait(barrier, n_tp - 1 + experts - 1)

    def tp_copy(src, dst, ssem, rsem, step):
        return pltpu.make_async_remote_copy(
            src_ref=src,
            dst_ref=dst,
            send_sem=ssem,
            recv_sem=rsem,
            device_id={"tp": tp_id(step)},
            device_id_type=MESH,
        )

    def arrival(dst, rsem):
        return pltpu.make_async_copy(dst, dst, rsem)

    sends = []
    for step in range(1, n_tp):
        for src, dst, ssem, rsem in (
            (hidden, hid_all, hid_ssem, hid_rsem),
            (moe_gain, gain_all, gain_ssem, gain_rsem),
        ):
            copy = tp_copy(src, dst.at[tp], ssem.at[step], rsem.at[tp], step)
            copy.start()
            sends.append(copy)
    for copy in local[2:5]:
        copy.start()
    kv_load.start()
    for copy in local[5:]:
        copy.start()

    kept = slots[...] < CAP
    aff = affinity[...]
    weight = route_scale * aff / jnp.sum(aff, -1, keepdims=True) * kept.astype(F32)
    target = jnp.where(kept, ids[...] * CAP + slots[...], -1)
    rows = experts * CAP
    iota = lax.broadcasted_iota(jnp.int32, (tokens, rows), 1)
    dispatch = jnp.zeros((tokens, rows), F32)
    combine = jnp.zeros((tokens, rows), F32)
    for k in range(ids.shape[1]):
        match = target[:, k : k + 1] == iota
        dispatch = jnp.where(match, 1.0, dispatch)
        combine = jnp.where(match, weight[:, k : k + 1], combine)
    dispatch = dispatch.T.astype(BF16)
    high = combine.astype(BF16)
    rest = combine - high.astype(F32)
    mid = rest.astype(BF16)
    low = (rest - mid.astype(F32)).astype(BF16)
    combine3 = jnp.concatenate([high, mid, low], 0)

    local[0].wait()
    local[1].wait()
    for step in range(1, n_tp):
        arrival(hid_all.at[tp_id(step)], hid_rsem.at[tp_id(step)]).wait()
        arrival(gain_all.at[tp_id(step)], gain_rsem.at[tp_id(step)]).wait()
    square = jnp.zeros((tokens, 1), F32)
    for b in range(n_tp):
        wide = hid_all[b].astype(F32)
        square = square + jnp.sum(wide * wide, -1, keepdims=True)
    scale = lax.rsqrt(square / d_all + epsilon)
    for b in range(n_tp):
        normed = (hid_all[b].astype(F32) * scale * gain_all[b]).astype(BF16)
        picked = jnp.dot(dispatch, normed, preferred_element_type=F32)
        send[:, b] = picked.reshape(experts, CAP, d_loc).astype(BF16)
    for step in range(1, experts):
        peer = ex_id(step)
        copy = pltpu.make_async_remote_copy(
            src_ref=send.at[peer],
            dst_ref=arrived.at[me],
            send_sem=row_ssem.at[step],
            recv_sem=row_rsem.at[me],
            device_id=ex_dev(peer),
            device_id_type=MESH,
        )
        copy.start()
        sends.append(copy)
    for g in range(GROUPS):
        span = pl.ds(g * per_group, per_group)
        for step in range(1, n_tp):
            copy = tp_copy(
                cache.at[span], kv_buf.at[span, tp], kv_ssem.at[step, g], kv_rsem.at[tp, g], step
            )
            copy.start()
            sends.append(copy)
    arrived[me] = send[me]

    local[2].wait()
    kv_load.wait()
    heads = queries.shape[1]
    span_len = cache.shape[1]
    total_len = n_tp * span_len

    def attend(g):
        span = pl.ds(g * per_group, per_group)
        for step in range(1, n_tp):
            arrival(kv_buf.at[span, tp_id(step)], kv_rsem.at[tp_id(step), g]).wait()

        def body(i, carry):
            t = g * per_group + i
            block = kv_buf[t].reshape(total_len, kvc)
            scores = (
                lax.dot_general(
                    q_buf[t], block, (((1,), (1,)), ((), ())), preferred_element_type=F32
                )
                * score_scale
            )
            live = lax.broadcasted_iota(jnp.int32, (heads, total_len), 1) < lengths[t]
            scores = jnp.where(live, scores, -1e30)
            peak = jnp.max(scores, -1, keepdims=True)
            prob = jnp.where(live, jnp.exp(scores - peak), 0.0)
            mass = jnp.sum(prob, -1, keepdims=True)
            acc[t] = jnp.dot(prob.astype(BF16), block[:, :lat], preferred_element_type=F32)
            peaks[t] = jnp.broadcast_to(peak, (heads, 128))
            masses[t] = jnp.broadcast_to(mass, (heads, 128))
            return carry

        lax.fori_loop(0, per_group, body, 0)

    attend(0)

    for step in range(1, experts):
        arrival(arrived.at[ex_id(step)], row_rsem.at[ex_id(step)]).wait()
    local[3].wait()
    local[4].wait()
    gate = jnp.zeros((rows, wg.shape[1]), F32)
    upper = jnp.zeros((rows, wg.shape[1]), F32)
    for b in range(n_tp):
        block = arrived[:, b].astype(F32).reshape(rows, d_loc).astype(BF16)
        gate = gate + jnp.dot(block, wg[b * d_loc : (b + 1) * d_loc], preferred_element_type=F32)
        upper = upper + jnp.dot(block, wu[b * d_loc : (b + 1) * d_loc], preferred_element_type=F32)
    units = (gate / (1.0 + jnp.exp(-gate)) * upper).astype(BF16)
    local[5].wait()
    width = 512 if d_all % 512 == 0 else 128
    for c in range(0, d_all, width):
        part = jnp.dot(units, wd[:, c : c + width], preferred_element_type=F32)
        ret_send[:, :, c : c + width] = part.reshape(experts, CAP, width).astype(BF16)
    for step in range(1, experts):
        peer = ex_id(step)
        copy = pltpu.make_async_remote_copy(
            src_ref=ret_send.at[peer],
            dst_ref=ret.at[me],
            send_sem=ret_ssem.at[step],
            recv_sem=ret_rsem.at[me],
            device_id=ex_dev(peer),
            device_id_type=MESH,
        )
        copy.start()
        sends.append(copy)
    ret[me] = ret_send[me]
    for g in range(1, GROUPS):
        attend(g)

    for step in range(1, experts):
        arrival(ret.at[ex_id(step)], ret_rsem.at[ex_id(step)]).wait()
    for c in range(0, d_all, width):
        block = ret[:, :, c : c + width].astype(F32).reshape(rows, width).astype(BF16)
        part = jnp.dot(combine3, block, preferred_element_type=F32)
        tsum[:, c : c + width] = part[:tokens] + (
            part[tokens : 2 * tokens] + part[2 * tokens : 3 * tokens]
        )
    for p in range(n_tp):
        rs_send[p] = tsum[:, p * d_loc : (p + 1) * d_loc].astype(BF16)
    for step in range(1, n_tp):
        copy = tp_copy(
            rs_send.at[tp_id(step)], rs_recv.at[tp], rs_ssem.at[step], rs_rsem.at[tp], step
        )
        copy.start()
        sends.append(copy)
    rs_recv[tp] = rs_send[tp]
    local[6].wait()
    for step in range(1, n_tp):
        arrival(rs_recv.at[tp_id(step)], rs_rsem.at[tp_id(step)]).wait()
    moe = rs_recv[0].astype(F32)
    for p in range(1, n_tp):
        moe = moe + rs_recv[p].astype(F32)
    next_hidden = (hid_all[tp].astype(F32) + moe).astype(BF16)
    next_out[...] = next_hidden
    next_wide = next_hidden.astype(F32)
    square = jnp.sum(next_wide * next_wide, -1, keepdims=True)
    scaled = (next_wide * attn_gain[...]).astype(BF16)
    kvp = up(kvc, 128)
    if kvp > kvc:
        key_send[:, kvp - 128 : kvp] = jnp.zeros((tokens, 128), F32)
    key_send[:, :kvc] = jnp.dot(scaled, wk[...], preferred_element_type=F32)
    key_send[:, kvp : kvp + 128] = jnp.broadcast_to(square, (tokens, 128))
    for step in range(1, n_tp):
        copy = tp_copy(key_send, key_recv.at[tp], key_ssem.at[step], key_rsem.at[tp], step)
        copy.start()
        sends.append(copy)
    key_recv[tp] = key_send[...]

    half = (kvc - lat) // 2
    lane = lax.broadcasted_iota(jnp.int32, (tokens, 2 * half), 1)
    pair = jnp.where(lane < half, lane, lane - half).astype(F32)
    freq = jnp.exp(pair * (-9.210340371976184 / half))
    row_id = lax.broadcasted_iota(jnp.int32, (tokens, 2 * half), 0)
    place = jnp.zeros((tokens, 2 * half), F32)
    for t in range(tokens):
        place = jnp.where(row_id == t, lengths[t].astype(F32), place)
    angle = place * freq
    cos_table = jnp.cos(angle)
    sin_table = jnp.where(lane < half, -1.0, 1.0) * jnp.sin(angle)

    for step in range(1, n_tp):
        arrival(key_recv.at[tp_id(step)], key_rsem.at[tp_id(step)]).wait()
    total = key_recv[0]
    for p in range(1, n_tp):
        total = total + key_recv[p]
    down = total * lax.rsqrt(total[:, kvp : kvp + 1] / d_all + epsilon)
    latent = down[:, :lat]
    latent = (
        latent
        * lax.rsqrt(jnp.mean(latent * latent, -1, keepdims=True) + epsilon)
        * kv_gain[...]
    )
    rope = down[:, lat:kvc]
    swapped = jnp.concatenate([rope[:, half:], rope[:, :half]], 1)
    rope = rope * cos_table + swapped * sin_table
    keys[:, :lat] = latent.astype(BF16).astype(F32)
    keys[:, lat:kvc] = rope.astype(BF16).astype(F32)

    def finish(t, carry):
        key = keys[pl.ds(t, 1), :]
        own = jnp.sum(q_buf[t].astype(F32) * key, -1, keepdims=True) * score_scale
        peak = peaks[t][:, :1]
        mass = masses[t][:, :1]
        top = jnp.maximum(peak, own)
        factor = jnp.exp(peak - top)
        own_prob = jnp.exp(own - top)
        inverse = 1.0 / (mass * factor + own_prob)
        own_b = own_prob.astype(BF16).astype(F32)
        latent_out[t] = (acc[t] * (factor * inverse) + (own_b * inverse) * key[:, :lat]).astype(
            BF16
        )
        return carry

    lax.fori_loop(0, tokens, finish, 0)
    for copy in sends:
        copy.wait_send()


def solution(mesh):
    n_tp, n_ep, n_mb = mesh.shape["tp"], mesh.shape["ep"], mesh.shape["mb"]
    experts = n_ep * n_mb

    def local(
        hidden,
        moe_gain,
        expert_ids,
        slots,
        affinity,
        w_gate,
        w_up,
        w_down,
        attn_gain,
        w_dkv,
        kv_gain,
        queries,
        cache,
        lengths,
    ):
        tokens, d_loc = hidden.shape
        d_all = d_loc * n_tp
        heads, kvc = queries.shape[1:]
        span = cache.shape[1]
        lat = kv_gain.shape[0]
        hid_dim = w_gate.shape[2]
        wide = up(kvc, 128) + 128
        any_space = pl.BlockSpec(memory_space=pl.ANY)
        vmem = pl.BlockSpec(memory_space=pltpu.VMEM)
        smem = pl.BlockSpec(memory_space=pltpu.SMEM)
        dma = pltpu.SemaphoreType.DMA
        return pl.pallas_call(
            functools.partial(kernel, n_tp, n_ep, n_mb),
            out_shape=(
                jax.ShapeDtypeStruct((tokens, d_loc), BF16),
                jax.ShapeDtypeStruct((tokens, heads, lat), BF16),
            ),
            in_specs=[
                any_space,
                any_space,
                vmem,
                vmem,
                vmem,
                any_space,
                any_space,
                any_space,
                vmem,
                any_space,
                vmem,
                any_space,
                any_space,
                smem,
            ],
            out_specs=(vmem, vmem),
            scratch_shapes=[
                pltpu.VMEM((n_tp, tokens, d_loc), BF16),
                pltpu.VMEM((n_tp, 1, d_loc), F32),
                pltpu.VMEM((experts, n_tp, CAP, d_loc), BF16),
                pltpu.VMEM((experts, n_tp, CAP, d_loc), BF16),
                pltpu.VMEM((d_all, hid_dim), BF16),
                pltpu.VMEM((d_all, hid_dim), BF16),
                pltpu.VMEM((hid_dim, d_all), BF16),
                pltpu.VMEM((d_loc, kvc), BF16),
                pltpu.VMEM((experts, CAP, d_all), BF16),
                pltpu.VMEM((experts, CAP, d_all), BF16),
                pltpu.VMEM((tokens, d_all), F32),
                pltpu.VMEM((n_tp, tokens, d_loc), BF16),
                pltpu.VMEM((n_tp, tokens, d_loc), BF16),
                pltpu.VMEM((tokens, wide), F32),
                pltpu.VMEM((n_tp, tokens, wide), F32),
                pltpu.VMEM((tokens, heads, kvc), BF16),
                pltpu.VMEM((tokens, n_tp, span, kvc), BF16),
                pltpu.VMEM((tokens, heads, lat), F32),
                pltpu.VMEM((tokens, heads, 128), F32),
                pltpu.VMEM((tokens, heads, 128), F32),
                pltpu.VMEM((tokens, kvc), F32),
                dma((7,)),
                dma,
                dma((n_tp,)),
                dma((n_tp,)),
                dma((n_tp,)),
                dma((n_tp,)),
                dma((n_tp, GROUPS)),
                dma((n_tp, GROUPS)),
                dma((experts,)),
                dma((experts,)),
                dma((experts,)),
                dma((experts,)),
                dma((n_tp,)),
                dma((n_tp,)),
                dma((n_tp,)),
                dma((n_tp,)),
            ],
            compiler_params=pltpu.CompilerParams(
                collective_id=0, has_side_effects=True, vmem_limit_bytes=60 * 1024 * 1024
            ),
        )(
            hidden,
            moe_gain[None],
            expert_ids,
            slots,
            affinity,
            w_gate,
            w_up,
            w_down,
            attn_gain[None],
            w_dkv,
            kv_gain[None],
            queries,
            cache,
            lengths,
        )

    return jax.shard_map(
        local,
        mesh=mesh,
        in_specs=(
            P(("grp", "ep", "mb"), "tp"),
            P("tp"),
            P(("grp", "ep", "mb"), None),
            P(("grp", "ep", "mb"), None),
            P(("grp", "ep", "mb"), None),
            P(("ep", "mb"), None, "tp"),
            P(("ep", "mb"), None, "tp"),
            P(("ep", "mb"), "tp", None),
            P("tp"),
            P("tp", None),
            P(),
            P(("grp", "ep", "mb"), "tp", None),
            P(("grp", "ep", "mb"), "tp", None),
            P(("grp", "ep", "mb")),
        ),
        out_specs=(P(("grp", "ep", "mb"), "tp"), P(("grp", "ep", "mb"), "tp", None)),
        check_vma=False,
    )
```

time: 116 us -> 68.5 us (0.59)
  Pallas kernels: 0 us -> 53.3 us
  blocking collectives: 29 us -> 0 us
  waiting for transfers between devices: 24 us -> 0 us
  starting transfers between devices: 19 us -> 0 us
  matrix products: 16.5 us -> 0 us
  between operations: 14.3 us -> 0.64 us
  local copies, waits for them, and re-layouts: 5.65 us -> 14.1 us
  other arithmetic: 6.73 us -> 0 us
    pallas_call x0 -> x1, Pallas kernels: none -> 53.3 us  [local(): pl.pallas_call(functools.partial(kernel, n_tp, n_ep, n_mb), out_shape=(ja...]
    psum x3 -> x0, blocking collectives: 24.1 us -> none  [the longest x1 11.2 us: local(): square_attn = lax.psum(jnp.sum(next_wide * next_wide, -1), 'tp')]
    all_to_all x5 -> x0, waiting for transfers between devices: 21 us -> none  [the longest x1 13 us: local(): lax.all_to_all(send_rows.reshape(experts, CAP, D), ('ep', 'mb'), split_ax...]
    all_to_all x5 -> x0, starting transfers between devices: 18.9 us -> none  [the longest x1 5.4 us: local(): lax.all_to_all(send_rows.reshape(experts, CAP, D), ('ep', 'mb'), split_ax...]
    dot_general x8 -> x0, matrix products: 16.5 us -> none  [the longest x1 5.39 us: local(): jnp.dot(units, down_weight, preferred_element_type=jnp.float32)]
    unnamed x22 -> x6, local copies, waits for them, and re-layouts: 3.17 us -> 11.5 us
    all_gather x1 -> x0, blocking collectives: 4.85 us -> none  [local(): full_rows = lax.all_gather(normed, 'tp', axis=1, tiled=True)]
    reduce_sum x8 -> x0, other arithmetic: 2.82 us -> none  [the longest x1 1.09 us: local(): square = lax.psum(jnp.sum(hidden_wide * hidden_wide, -1), 'tp')]
  transfers between devices with their start and end apart: 7 -> 0, of which waited for: 4 -> 0; matrix products, arithmetic and copies ran while one was open for 20% -> 0% of each run, Pallas kernels for 0% -> 0%
where the time goes in v1:
time: 68.5 us; the launch traced here: 68 us
  Pallas kernels  53.3 us (78%)
  local copies, waits for them, and re-layouts  14.1 us (21%)
    pallas_call x1, Pallas kernels, local(): pl.pallas_call(functools.partial(kernel, n_tp, n_ep, n_mb), out_shape=(ja...  53.3 us
    unnamed x6, local copies, waits for them, and re-layouts  11.5 us

profile of v1, /device:TPU:0, one launch (start us, length us, event | category | flops | bytes accessed | tf_op | source)
XLA Modules:
  0.0 68.0 jit_solution(14775040813002047406)
XLA Ops:
  0.6 1.3 %broadcast_in_dim.9.moe_gain = f32[1,1792]{1,0:T(1,128)} reshape(f32[1792]{0:T(1024)} %param.15) | data formatting | bytes 14336 | tf_op jit(solution)/shard_map/broadcast_in_dim | solution.py:456
  1.9 1.3 %broadcast_in_dim.10.attn_gain = f32[1,1792]{1,0:T(1,128)} reshape(f32[1792]{0:T(1024)} %param.22) | data formatting | bytes 14336 | tf_op jit(solution)/shard_map/broadcast_in_dim | solution.py:463
  3.2 1.4 %copy.16.ids = s32[16,8]{1,0:T(8,128)} copy(s32[16,8]{0,1:T(8,128)} %param.16) | data formatting | bytes 1024 | tf_op args[2]
  4.6 1.4 %copy.17.slots = s32[16,8]{1,0:T(8,128)} copy(s32[16,8]{0,1:T(8,128)} %param.17) | data formatting | bytes 1024 | tf_op args[3]
  5.9 1.3 %copy.18.affinity = f32[16,8]{1,0:T(8,128)} copy(f32[16,8]{0,1:T(8,128)} %param.18) | data formatting | bytes 1024 | tf_op args[4]
  7.3 4.1 %copy.19.w_dkv = bf16[1792,576]{1,0:T(8,128)(2,1)} copy(bf16[1792,576]{0,1:T(8,128)(2,1)} %param.23) | data formatting | bytes 4128768 | tf_op args[9]
  11.4 53.3 %shard_map.149 = (bf16[16,1792]{1,0:T(8,128)(2,1)}, bf16[16,32,512]{2,1,0:T(8,128)(2,1)}) custom-call(bf16[16,1792]{1,0:T(8,128)(2,1)} %hidden.1, f32[1,1792]{1,0:T(1,128)} %broadcast_in_dim.9.moe_gain, s32[16,8]{1,0:T(8,128)} %copy.16.ids, s32[16,8]{1,0:T(8,128)} %copy.17.slots, f32[16,8]{1,0:T(8,128)} %copy.18.affinity, bf16[1,3584,512]{2,1,0:T(8,128)(2,1)} %w_gate.1, ...), custom_call_target="tpu_custom_call" | custom-call | tf_op jit(solution)/shard_map/pallas_call | solution.py:389
  64.7 1.4 %copy.22 = bf16[16,1792]{1,0:T(8,128)(2,1)} copy(bf16[16,1792]{1,0:T(8,128)(2,1)} %get-tuple-element.4) | data formatting | bytes 114688
  66.1 1.9 %copy.23 = bf16[16,32,512]{2,1,0:T(8,128)(2,1)} copy(bf16[16,32,512]{2,1,0:T(8,128)(2,1)} %get-tuple-element.5) | data formatting | bytes 1048576

commit v2 on v1

--- a/solution.py
+++ b/solution.py
@@ -99,16 +99,15 @@
 
     local = [
         pltpu.make_async_copy(hidden, hid_all.at[tp], load_sem.at[0]),
-        pltpu.make_async_copy(moe_gain, gain_all.at[tp], load_sem.at[1]),
-        pltpu.make_async_copy(queries, q_buf, load_sem.at[2]),
-        pltpu.make_async_copy(w_gate.at[0], wg, load_sem.at[3]),
-        pltpu.make_async_copy(w_up.at[0], wu, load_sem.at[4]),
-        pltpu.make_async_copy(w_down.at[0], wd, load_sem.at[5]),
-        pltpu.make_async_copy(w_dkv, wk, load_sem.at[6]),
+        pltpu.make_async_copy(queries, q_buf, load_sem.at[1]),
+        pltpu.make_async_copy(w_gate.at[0], wg, load_sem.at[2]),
+        pltpu.make_async_copy(w_up.at[0], wu, load_sem.at[3]),
+        pltpu.make_async_copy(w_down.at[0], wd, load_sem.at[4]),
+        pltpu.make_async_copy(w_dkv, wk, load_sem.at[5]),
     ]
     kv_load = pltpu.make_async_copy(cache, kv_buf.at[:, tp], kv_load_sem)
     local[0].start()
-    local[1].start()
+    gain_all[tp] = moe_gain[...].reshape(1, d_loc)
 
     barrier = pltpu.get_barrier_semaphore()
     for step in range(1, n_tp):
@@ -134,30 +133,31 @@
     for step in range(1, n_tp):
         for src, dst, ssem, rsem in (
             (hidden, hid_all, hid_ssem, hid_rsem),
-            (moe_gain, gain_all, gain_ssem, gain_rsem),
+            (gain_all.at[tp], gain_all, gain_ssem, gain_rsem),
         ):
             copy = tp_copy(src, dst.at[tp], ssem.at[step], rsem.at[tp], step)
             copy.start()
             sends.append(copy)
-    for copy in local[2:5]:
+    for copy in local[1:4]:
         copy.start()
     kv_load.start()
-    for copy in local[5:]:
+    for copy in local[4:]:
         copy.start()
 
     kept = slots[...] < CAP
     aff = affinity[...]
-    weight = route_scale * aff / jnp.sum(aff, -1, keepdims=True) * kept.astype(F32)
+    weight = route_scale * aff / jnp.sum(aff, 0, keepdims=True) * kept.astype(F32)
     target = jnp.where(kept, ids[...] * CAP + slots[...], -1)
     rows = experts * CAP
-    iota = lax.broadcasted_iota(jnp.int32, (tokens, rows), 1)
-    dispatch = jnp.zeros((tokens, rows), F32)
-    combine = jnp.zeros((tokens, rows), F32)
-    for k in range(ids.shape[1]):
-        match = target[:, k : k + 1] == iota
+    iota = lax.broadcasted_iota(jnp.int32, (rows, tokens), 0)
+    dispatch = jnp.zeros((rows, tokens), F32)
+    combine = jnp.zeros((rows, tokens), F32)
+    for k in range(ids.shape[0]):
+        match = target[k : k + 1] == iota
         dispatch = jnp.where(match, 1.0, dispatch)
-        combine = jnp.where(match, weight[:, k : k + 1], combine)
-    dispatch = dispatch.T.astype(BF16)
+        combine = jnp.where(match, weight[k : k + 1], combine)
+    dispatch = dispatch.astype(BF16)
+    combine = combine.T
     high = combine.astype(BF16)
     rest = combine - high.astype(F32)
     mid = rest.astype(BF16)
@@ -165,10 +165,17 @@
     combine3 = jnp.concatenate([high, mid, low], 0)
 
     local[0].wait()
-    local[1].wait()
     for step in range(1, n_tp):
         arrival(hid_all.at[tp_id(step)], hid_rsem.at[tp_id(step)]).wait()
         arrival(gain_all.at[tp_id(step)], gain_rsem.at[tp_id(step)]).wait()
+    for g in range(GROUPS):
+        span = pl.ds(g * per_group, per_group)
+        for step in range(1, n_tp):
+            copy = tp_copy(
+                cache.at[span], kv_buf.at[span, tp], kv_ssem.at[step, g], kv_rsem.at[tp, g], step
+            )
+            copy.start()
+            sends.append(copy)
     square = jnp.zeros((tokens, 1), F32)
     for b in range(n_tp):
         wide = hid_all[b].astype(F32)
@@ -190,17 +197,9 @@
         )
         copy.start()
         sends.append(copy)
-    for g in range(GROUPS):
-        span = pl.ds(g * per_group, per_group)
-        for step in range(1, n_tp):
-            copy = tp_copy(
-                cache.at[span], kv_buf.at[span, tp], kv_ssem.at[step, g], kv_rsem.at[tp, g], step
-            )
-            copy.start()
-            sends.append(copy)
     arrived[me] = send[me]
 
-    local[2].wait()
+    local[1].wait()
     kv_load.wait()
     heads = queries.shape[1]
     span_len = cache.shape[1]
@@ -232,12 +231,10 @@
 
         lax.fori_loop(0, per_group, body, 0)
 
-    attend(0)
-
     for step in range(1, experts):
         arrival(arrived.at[ex_id(step)], row_rsem.at[ex_id(step)]).wait()
+    local[2].wait()
     local[3].wait()
-    local[4].wait()
     gate = jnp.zeros((rows, wg.shape[1]), F32)
     upper = jnp.zeros((rows, wg.shape[1]), F32)
     for b in range(n_tp):
@@ -245,35 +242,38 @@
         gate = gate + jnp.dot(block, wg[b * d_loc : (b + 1) * d_loc], preferred_element_type=F32)
         upper = upper + jnp.dot(block, wu[b * d_loc : (b + 1) * d_loc], preferred_element_type=F32)
     units = (gate / (1.0 + jnp.exp(-gate)) * upper).astype(BF16)
-    local[5].wait()
+    local[4].wait()
     width = 512 if d_all % 512 == 0 else 128
-    for c in range(0, d_all, width):
-        part = jnp.dot(units, wd[:, c : c + width], preferred_element_type=F32)
-        ret_send[:, :, c : c + width] = part.reshape(experts, CAP, width).astype(BF16)
-    for step in range(1, experts):
-        peer = ex_id(step)
-        copy = pltpu.make_async_remote_copy(
-            src_ref=ret_send.at[peer],
-            dst_ref=ret.at[me],
-            send_sem=ret_ssem.at[step],
-            recv_sem=ret_rsem.at[me],
-            device_id=ex_dev(peer),
-            device_id_type=MESH,
-        )
-        copy.start()
-        sends.append(copy)
+    middle = d_all // width // 2 * width
+    halves = [(0, middle), (middle, d_all)]
+    for h, (first, last) in enumerate(halves):
+        for c in range(first, last, width):
+            part = jnp.dot(units, wd[:, c : c + width], preferred_element_type=F32)
+            ret_send[:, :, c : c + width] = part.reshape(experts, CAP, width).astype(BF16)
+        for step in range(1, experts):
+            peer = ex_id(step)
+            copy = pltpu.make_async_remote_copy(
+                src_ref=ret_send.at[peer, :, first:last],
+                dst_ref=ret.at[me, :, first:last],
+                send_sem=ret_ssem.at[step, h],
+                recv_sem=ret_rsem.at[me, h],
+                device_id=ex_dev(peer),
+                device_id_type=MESH,
+            )
+            copy.start()
+            sends.append(copy)
     ret[me] = ret_send[me]
-    for g in range(1, GROUPS):
-        attend(g)
-
-    for step in range(1, experts):
-        arrival(ret.at[ex_id(step)], ret_rsem.at[ex_id(step)]).wait()
-    for c in range(0, d_all, width):
-        block = ret[:, :, c : c + width].astype(F32).reshape(rows, width).astype(BF16)
-        part = jnp.dot(combine3, block, preferred_element_type=F32)
-        tsum[:, c : c + width] = part[:tokens] + (
-            part[tokens : 2 * tokens] + part[2 * tokens : 3 * tokens]
-        )
+
+    for h, (first, last) in enumerate(halves):
+        for step in range(1, experts):
+            peer = ex_id(step)
+            arrival(ret.at[peer, :, first:last], ret_rsem.at[peer, h]).wait()
+        for c in range(first, last, width):
+            block = ret[:, :, c : c + width].astype(F32).reshape(rows, width).astype(BF16)
+            part = jnp.dot(combine3, block, preferred_element_type=F32)
+            tsum[:, c : c + width] = part[:tokens] + (
+                part[tokens : 2 * tokens] + part[2 * tokens : 3 * tokens]
+            )
     for p in range(n_tp):
         rs_send[p] = tsum[:, p * d_loc : (p + 1) * d_loc].astype(BF16)
     for step in range(1, n_tp):
@@ -283,7 +283,9 @@
         copy.start()
         sends.append(copy)
     rs_recv[tp] = rs_send[tp]
-    local[6].wait()
+    for g in range(GROUPS // 2):
+        attend(g)
+    local[5].wait()
     for step in range(1, n_tp):
         arrival(rs_recv.at[tp_id(step)], rs_rsem.at[tp_id(step)]).wait()
     moe = rs_recv[0].astype(F32)
@@ -293,17 +295,21 @@
     next_out[...] = next_hidden
     next_wide = next_hidden.astype(F32)
     square = jnp.sum(next_wide * next_wide, -1, keepdims=True)
-    scaled = (next_wide * attn_gain[...]).astype(BF16)
+    scaled = (next_wide * attn_gain[...].reshape(1, d_loc)).astype(BF16)
     kvp = up(kvc, 128)
     if kvp > kvc:
         key_send[:, kvp - 128 : kvp] = jnp.zeros((tokens, 128), F32)
-    key_send[:, :kvc] = jnp.dot(scaled, wk[...], preferred_element_type=F32)
+    key_send[:, :kvc] = lax.dot_general(
+        scaled, wk[...], (((1,), (1,)), ((), ())), preferred_element_type=F32
+    )
     key_send[:, kvp : kvp + 128] = jnp.broadcast_to(square, (tokens, 128))
     for step in range(1, n_tp):
         copy = tp_copy(key_send, key_recv.at[tp], key_ssem.at[step], key_rsem.at[tp], step)
         copy.start()
         sends.append(copy)
     key_recv[tp] = key_send[...]
+    for g in range(GROUPS // 2, GROUPS):
+        attend(g)
 
     half = (kvc - lat) // 2
     lane = lax.broadcasted_iota(jnp.int32, (tokens, 2 * half), 1)
@@ -394,7 +400,7 @@
             ),
             in_specs=[
                 any_space,
-                any_space,
+                vmem,
                 vmem,
                 vmem,
                 vmem,
@@ -417,7 +423,7 @@
                 pltpu.VMEM((d_all, hid_dim), BF16),
                 pltpu.VMEM((d_all, hid_dim), BF16),
                 pltpu.VMEM((hid_dim, d_all), BF16),
-                pltpu.VMEM((d_loc, kvc), BF16),
+                pltpu.VMEM((kvc, d_loc), BF16),
                 pltpu.VMEM((experts, CAP, d_all), BF16),
                 pltpu.VMEM((experts, CAP, d_all), BF16),
                 pltpu.VMEM((tokens, d_all), F32),
@@ -431,7 +437,7 @@
                 pltpu.VMEM((tokens, heads, 128), F32),
                 pltpu.VMEM((tokens, heads, 128), F32),
                 pltpu.VMEM((tokens, kvc), F32),
-                dma((7,)),
+                dma((6,)),
                 dma,
                 dma((n_tp,)),
                 dma((n_tp,)),
@@ -441,8 +447,8 @@
                 dma((n_tp, GROUPS)),
                 dma((experts,)),
                 dma((experts,)),
-                dma((experts,)),
-                dma((experts,)),
+                dma((experts, 2)),
+                dma((experts, 2)),
                 dma((n_tp,)),
                 dma((n_tp,)),
                 dma((n_tp,)),
@@ -453,15 +459,15 @@
             ),
         )(
             hidden,
-            moe_gain[None],
-            expert_ids,
-            slots,
-            affinity,
+            moe_gain,
+            expert_ids.T,
+            slots.T,
+            affinity.T,
             w_gate,
             w_up,
             w_down,
-            attn_gain[None],
-            w_dkv,
+            attn_gain,
+            w_dkv.T,
             kv_gain[None],
             queries,
             cache,

time: 68.5 us -> 54.1 us (0.79)
  local copies, waits for them, and re-layouts: 14.1 us -> 3.33 us
  Pallas kernels: 53.3 us -> 49.9 us
    unnamed x6 -> x2, local copies, waits for them, and re-layouts: 11.5 us -> 3.33 us
    pallas_call x1, Pallas kernels: 53.3 us -> 49.9 us  [local(): pl.pallas_call(functools.partial(kernel, n_tp, n_ep, n_mb), out_shape=(ja...]
    broadcast_in_dim x2 -> x0, local copies, waits for them, and re-layouts: 2.59 us -> none  [the longest x1 1.3 us: local(): moe_gain[None]]
where the time goes in v2:
time: 54.1 us; the launch traced here: 53.8 us
  Pallas kernels  49.9 us (92%)
  local copies, waits for them, and re-layouts  3.33 us (6%)
  between operations  0.64 us (1%)
    pallas_call x1, Pallas kernels, local(): pl.pallas_call(functools.partial(kernel, n_tp, n_ep, n_mb), out_shape=(ja...  49.9 us
    unnamed x2, local copies, waits for them, and re-layouts  3.33 us

profile of v2, /device:TPU:0, one launch (start us, length us, event | category | flops | bytes accessed | tf_op | source)
XLA Modules:
  0.0 53.8 jit_solution(14854072259243862290)
XLA Ops:
  0.6 49.9 %shard_map.149 = (bf16[16,1792]{1,0:T(8,128)(2,1)}, bf16[16,32,512]{2,1,0:T(8,128)(2,1)}) custom-call(bf16[16,1792]{1,0:T(8,128)(2,1)} %hidden.1, f32[1792]{0:T(1024)} %moe_gain.1, s32[8,16]{1,0:T(8,128)} %bitcast.6, s32[8,16]{1,0:T(8,128)} %bitcast.7, f32[8,16]{1,0:T(8,128)} %bitcast.8, bf16[1,3584,512]{2,1,0:T(8,128)(2,1)} %w_gate.1, ...), custom_call_target="tpu_custom_call" | custom-call | tf_op jit(solution)/shard_map/pallas_call | solution.py:395
  50.5 1.4 %copy.18 = bf16[16,1792]{1,0:T(8,128)(2,1)} copy(bf16[16,1792]{1,0:T(8,128)(2,1)} %get-tuple-element.4) | data formatting | bytes 114688
  52.0 1.9 %copy.19 = bf16[16,32,512]{2,1,0:T(8,128)(2,1)} copy(bf16[16,32,512]{2,1,0:T(8,128)(2,1)} %get-tuple-element.5) | data formatting | bytes 1048576

commit v3 on v2

--- a/solution.py
+++ b/solution.py
@@ -114,36 +114,6 @@
         pl.semaphore_signal(barrier, inc=1, device_id={"tp": tp_id(step)}, device_id_type=MESH)
     for step in range(1, experts):
         pl.semaphore_signal(barrier, inc=1, device_id=ex_dev(ex_id(step)), device_id_type=MESH)
-    pl.semaphore_wait(barrier, n_tp - 1 + experts - 1)
-
-    def tp_copy(src, dst, ssem, rsem, step):
-        return pltpu.make_async_remote_copy(
-            src_ref=src,
-            dst_ref=dst,
-            send_sem=ssem,
-            recv_sem=rsem,
-            device_id={"tp": tp_id(step)},
-            device_id_type=MESH,
-        )
-
-    def arrival(dst, rsem):
-        return pltpu.make_async_copy(dst, dst, rsem)
-
-    sends = []
-    for step in range(1, n_tp):
-        for src, dst, ssem, rsem in (
-            (hidden, hid_all, hid_ssem, hid_rsem),
-            (gain_all.at[tp], gain_all, gain_ssem, gain_rsem),
-        ):
-            copy = tp_copy(src, dst.at[tp], ssem.at[step], rsem.at[tp], step)
-            copy.start()
-            sends.append(copy)
-    for copy in local[1:4]:
-        copy.start()
-    kv_load.start()
-    for copy in local[4:]:
-        copy.start()
-
     kept = slots[...] < CAP
     aff = affinity[...]
     weight = route_scale * aff / jnp.sum(aff, 0, keepdims=True) * kept.astype(F32)
@@ -164,10 +134,52 @@
     low = (rest - mid.astype(F32)).astype(BF16)
     combine3 = jnp.concatenate([high, mid, low], 0)
 
+    def pick(block):
+        picked = jnp.dot(dispatch, hid_all[block], preferred_element_type=F32)
+        send[:, block] = picked.reshape(experts, CAP, d_loc).astype(BF16)
+
+    def ship(block, turn):
+        for step in range(1, experts):
+            peer = ex_id(step)
+            copy = pltpu.make_async_remote_copy(
+                src_ref=send.at[peer, block],
+                dst_ref=arrived.at[me, block],
+                send_sem=row_ssem.at[step, turn],
+                recv_sem=row_rsem.at[me, block],
+                device_id=ex_dev(peer),
+                device_id_type=MESH,
+            )
+            copy.start()
+            sends.append(copy)
+        arrived[me, block] = send[me, block]
+
     local[0].wait()
+    pick(tp)
+    pl.semaphore_wait(barrier, n_tp - 1 + experts - 1)
+
+    def tp_copy(src, dst, ssem, rsem, step):
+        return pltpu.make_async_remote_copy(
+            src_ref=src,
+            dst_ref=dst,
+            send_sem=ssem,
+            recv_sem=rsem,
+            device_id={"tp": tp_id(step)},
+            device_id_type=MESH,
+        )
+
+    def arrival(dst, rsem):
+        return pltpu.make_async_copy(dst, dst, rsem)
+
+    sends = []
     for step in range(1, n_tp):
-        arrival(hid_all.at[tp_id(step)], hid_rsem.at[tp_id(step)]).wait()
-        arrival(gain_all.at[tp_id(step)], gain_rsem.at[tp_id(step)]).wait()
+        for src, dst, ssem, rsem in (
+            (hidden, hid_all, hid_ssem, hid_rsem),
+            (gain_all.at[tp], gain_all, gain_ssem, gain_rsem),
+        ):
+            copy = tp_copy(src, dst.at[tp], ssem.at[step], rsem.at[tp], step)
+            copy.start()
+            sends.append(copy)
+    ship(tp, 0)
     for g in range(GROUPS):
         span = pl.ds(g * per_group, per_group)
         for step in range(1, n_tp):
@@ -176,28 +188,18 @@
             )
             copy.start()
             sends.append(copy)
-    square = jnp.zeros((tokens, 1), F32)
-    for b in range(n_tp):
-        wide = hid_all[b].astype(F32)
-        square = square + jnp.sum(wide * wide, -1, keepdims=True)
-    scale = lax.rsqrt(square / d_all + epsilon)
-    for b in range(n_tp):
-        normed = (hid_all[b].astype(F32) * scale * gain_all[b]).astype(BF16)
-        picked = jnp.dot(dispatch, normed, preferred_element_type=F32)
-        send[:, b] = picked.reshape(experts, CAP, d_loc).astype(BF16)
-    for step in range(1, experts):
-        peer = ex_id(step)
-        copy = pltpu.make_async_remote_copy(
-            src_ref=send.at[peer],
-            dst_ref=arrived.at[me],
-            send_sem=row_ssem.at[step],
-            recv_sem=row_rsem.at[me],
-            device_id=ex_dev(peer),
-            device_id_type=MESH,
-        )
+    for copy in local[1:4]:
         copy.start()
-        sends.append(copy)
-    arrived[me] = send[me]
+    kv_load.start()
+    for copy in local[4:]:
+        copy.start()
+
+    for step in range(1, n_tp):
+        arrival(hid_all.at[tp_id(step)], hid_rsem.at[tp_id(step)]).wait()
+        arrival(gain_all.at[tp_id(step)], gain_rsem.at[tp_id(step)]).wait()
+    for turn in range(1, n_tp):
+        pick(tp_id(turn))
+        ship(tp_id(turn), turn)
 
     local[1].wait()
     kv_load.wait()
@@ -231,30 +233,52 @@
 
         lax.fori_loop(0, per_group, body, 0)
 
-    for step in range(1, experts):
-        arrival(arrived.at[ex_id(step)], row_rsem.at[ex_id(step)]).wait()
     local[2].wait()
     local[3].wait()
     gate = jnp.zeros((rows, wg.shape[1]), F32)
     upper = jnp.zeros((rows, wg.shape[1]), F32)
-    for b in range(n_tp):
-        block = arrived[:, b].astype(F32).reshape(rows, d_loc).astype(BF16)
-        gate = gate + jnp.dot(block, wg[b * d_loc : (b + 1) * d_loc], preferred_element_type=F32)
-        upper = upper + jnp.dot(block, wu[b * d_loc : (b + 1) * d_loc], preferred_element_type=F32)
+    square = jnp.zeros((rows, 1), F32)
+    for turn in range(n_tp):
+        b = tp_id(turn)
+        for step in range(1, experts):
+            peer = ex_id(step)
+            arrival(arrived.at[peer, b], row_rsem.at[peer, b]).wait()
+        wide = arrived[:, b].astype(F32).reshape(rows, d_loc)
+        square = square + jnp.sum(wide * wide, -1, keepdims=True)
+        block = (wide * gain_all[b]).astype(BF16)
+        deep = pl.ds(pl.multiple_of(b * d_loc, d_loc & -d_loc), d_loc)
+        gate = gate + jnp.dot(block, wg[deep], preferred_element_type=F32)
+        upper = upper + jnp.dot(block, wu[deep], preferred_element_type=F32)
+    scale = lax.rsqrt(square / d_all + epsilon)
+    gate = gate * scale
+    upper = upper * scale
     units = (gate / (1.0 + jnp.exp(-gate)) * upper).astype(BF16)
     local[4].wait()
     width = 512 if d_all % 512 == 0 else 128
-    middle = d_all // width // 2 * width
-    halves = [(0, middle), (middle, d_all)]
-    for h, (first, last) in enumerate(halves):
-        for c in range(first, last, width):
-            part = jnp.dot(units, wd[:, c : c + width], preferred_element_type=F32)
-            ret_send[:, :, c : c + width] = part.reshape(experts, CAP, width).astype(BF16)
+    aligned = d_loc % 128 == 0
+    if aligned:
+        width = next(w for w in (896, 512, 384, 256, 128) if d_loc % w == 0)
+        pieces = [
+            (pl.multiple_of(tp_id(turn) * d_loc, 128), d_loc) for turn in (*range(1, n_tp), 0)
+        ]
+    else:
+        middle = d_all // width // 2 * width
+        pieces = [(0, middle), (middle, d_all - middle)]
+
+    def columns(start, size):
+        return pl.ds(pl.multiple_of(start, 128), size)
+
+    for h, (first, size) in enumerate(pieces):
+        for c in range(0, size, width):
+            part = jnp.dot(units, wd[:, columns(first + c, width)], preferred_element_type=F32)
+            ret_send[:, :, columns(first + c, width)] = part.reshape(
+                experts, CAP, width
+            ).astype(BF16)
         for step in range(1, experts):
             peer = ex_id(step)
             copy = pltpu.make_async_remote_copy(
-                src_ref=ret_send.at[peer, :, first:last],
-                dst_ref=ret.at[me, :, first:last],
+                src_ref=ret_send.at[peer, :, columns(first, size)],
+                dst_ref=ret.at[me, :, columns(first, size)],
                 send_sem=ret_ssem.at[step, h],
                 recv_sem=ret_rsem.at[me, h],
                 device_id=ex_dev(peer),
@@ -264,27 +288,37 @@
             sends.append(copy)
     ret[me] = ret_send[me]
 
-    for h, (first, last) in enumerate(halves):
-        for step in range(1, experts):
-            peer = ex_id(step)
-            arrival(ret.at[peer, :, first:last], ret_rsem.at[peer, h]).wait()
-        for c in range(first, last, width):
-            block = ret[:, :, c : c + width].astype(F32).reshape(rows, width).astype(BF16)
-            part = jnp.dot(combine3, block, preferred_element_type=F32)
-            tsum[:, c : c + width] = part[:tokens] + (
-                part[tokens : 2 * tokens] + part[2 * tokens : 3 * tokens]
-            )
-    for p in range(n_tp):
-        rs_send[p] = tsum[:, p * d_loc : (p + 1) * d_loc].astype(BF16)
-    for step in range(1, n_tp):
+    def exchange(step):
         copy = tp_copy(
             rs_send.at[tp_id(step)], rs_recv.at[tp], rs_ssem.at[step], rs_rsem.at[tp], step
         )
         copy.start()
         sends.append(copy)
+
+    for h, (first, size) in enumerate(pieces):
+        for step in range(1, experts):
+            peer = ex_id(step)
+            arrival(ret.at[peer, :, columns(first, size)], ret_rsem.at[peer, h]).wait()
+        for c in range(0, size, width):
+            block = ret[:, :, columns(first + c, width)].astype(F32)
+            block = block.reshape(rows, width).astype(BF16)
+            part = jnp.dot(combine3, block, preferred_element_type=F32)
+            part = part[:tokens] + (part[tokens : 2 * tokens] + part[2 * tokens : 3 * tokens])
+            if aligned:
+                rs_send[tp_id(h + 1), :, c : c + width] = part.astype(BF16)
+            else:
+                tsum[:, columns(first + c, width)] = part
+        if aligned and h < n_tp - 1:
+            exchange(h + 1)
+        if h == 0:
+            for g in range(GROUPS // 2):
+                attend(g)
+    if not aligned:
+        for p in range(n_tp):
+            rs_send[p] = tsum[:, p * d_loc : (p + 1) * d_loc].astype(BF16)
+        for step in range(1, n_tp):
+            exchange(step)
     rs_recv[tp] = rs_send[tp]
-    for g in range(GROUPS // 2):
-        attend(g)
     local[5].wait()
     for step in range(1, n_tp):
         arrival(rs_recv.at[tp_id(step)], rs_rsem.at[tp_id(step)]).wait()
@@ -445,10 +479,10 @@
                 dma((n_tp,)),
                 dma((n_tp, GROUPS)),
                 dma((n_tp, GROUPS)),
-                dma((experts,)),
-                dma((experts,)),
-                dma((experts, 2)),
-                dma((experts, 2)),
+                dma((experts, n_tp)),
+                dma((experts, n_tp)),
+                dma((experts, max(2, n_tp))),
+                dma((experts, max(2, n_tp))),
                 dma((n_tp,)),
                 dma((n_tp,)),
                 dma((n_tp,)),

time: 54.1 us -> 52.9 us (0.978)
  Pallas kernels: 49.9 us -> 48.6 us
    pallas_call x1, Pallas kernels: 49.9 us -> 48.6 us  [local(): pl.pallas_call(functools.partial(kernel, n_tp, n_ep, n_mb), out_shape=(ja...]
where the time goes in v3:
time: 52.9 us; the launch traced here: 52.6 us
  Pallas kernels  48.6 us (92%)
  local copies, waits for them, and re-layouts  3.33 us (6%)
  between operations  0.64 us (1%)
    pallas_call x1, Pallas kernels, local(): pl.pallas_call(functools.partial(kernel, n_tp, n_ep, n_mb), out_shape=(ja...  48.6 us
    unnamed x2, local copies, waits for them, and re-layouts  3.33 us

profile of v3, /device:TPU:0, one launch (start us, length us, event | category | flops | bytes accessed | tf_op | source)
XLA Modules:
  0.0 52.6 jit_solution(12637204748209121876)
XLA Ops:
  0.6 48.6 %shard_map.149 = (bf16[16,1792]{1,0:T(8,128)(2,1)}, bf16[16,32,512]{2,1,0:T(8,128)(2,1)}) custom-call(bf16[16,1792]{1,0:T(8,128)(2,1)} %hidden.1, f32[1792]{0:T(1024)} %moe_gain.1, s32[8,16]{1,0:T(8,128)} %bitcast.6, s32[8,16]{1,0:T(8,128)} %bitcast.7, f32[8,16]{1,0:T(8,128)} %bitcast.8, bf16[1,3584,512]{2,1,0:T(8,128)(2,1)} %w_gate.1, ...), custom_call_target="tpu_custom_call" | custom-call | tf_op jit(solution)/shard_map/pallas_call | solution.py:429
  49.3 1.4 %copy.18 = bf16[16,1792]{1,0:T(8,128)(2,1)} copy(bf16[16,1792]{1,0:T(8,128)(2,1)} %get-tuple-element.4) | data formatting | bytes 114688
  50.7 1.9 %copy.19 = bf16[16,32,512]{2,1,0:T(8,128)(2,1)} copy(bf16[16,32,512]{2,1,0:T(8,128)(2,1)} %get-tuple-element.5) | data formatting | bytes 1048576
